TPU v7x, 512 devices: a whole 4x4x16 slice. The times are simulated.
512 devices in a mesh: dp: 32 (over y_hi, z), tm: 16 (over y_lo, x, core).
Axes of the slice: x: 4, y: 4 (y_hi: 2, y_lo: 2; y = y_hi * 2 + y_lo), z: 16, core: 2. Of those that a mesh axis runs over, the one named last changes fastest.
Arguments:
- frames: bfloat16 [32, 4096, 1536], P('dp', 'tm'), may hold values from -6 to 6
- lengths: int32 [32], P('dp'), may hold values from 1024 to 4096
- ln_gain: float32 [1536], replicated, may hold values from 0.1 to 1.9
- w_query: bfloat16 [1536, 768], P('dp'), may hold values from -0.15625 to 0.15625
- w_key: bfloat16 [1536, 768], P('dp'), may hold values from -0.15625 to 0.15625
- w_value: bfloat16 [1536, 768], P('dp'), may hold values from -0.15625 to 0.15625
- w_output: bfloat16 [768, 1536], P('dp'), may hold values from -0.21875 to 0.21875
- w_position: bfloat16 [1536, 768], P(None, 'tm'), may hold values from -0.15625 to 0.15625
- bias_content: float32 [8, 96], replicated, may hold values from -60 to 60, as said below
- bias_position: float32 [8, 96], replicated, may hold values from -3 to 3
Outputs:
- attended: bfloat16 [32, 4096, 1536], P('dp', 'tm')
Inputs may be any that keep to these rules, and one draw needn't show every extreme that they name: `lengths`: number of valid frames of each utterance; later frames are padding. `bias_content`: content biases; in some draws they reach magnitudes near 60.
All inputs are finite; a program needn't handle non-finite values.
Results may differ from a plain program's by a relative error of at most 0.012.
The roundings to bfloat16 on the way count: a program that leaves them out, or rounds other values in their place, can miss the bound.
Values may be sent and summed in bfloat16 or wider, within the bound.
A program may use at most 64 MiB of HBM per device.

v0:
```python
import math

import jax
import jax.numpy as jnp
from jax import lax
from jax.sharding import PartitionSpec as P

epsilon = 1e-05
masked_score = -1e30


def from_everyone(value, axis):
    size = lax.axis_size(axis)
    return lax.all_to_all(
        jnp.broadcast_to(value[None], (size, *value.shape)), axis, 0, 0, tiled=True
    )


def laid_out(parts, dim):
    lengths = list(parts.shape[1:])
    lengths[dim] *= parts.shape[0]
    return jnp.moveaxis(parts, 0, dim).reshape(lengths)


def gathered_copies(value, axis, dim):
    parts = from_everyone(value, axis)
    return laid_out(parts, dim)


def padded(block, sides, width):
    for axis, dim in sides:
        count = lax.axis_size(axis)
        forward = [(i, i + 1) for i in range(count - 1)]
        backward = [(target, source) for source, target in forward]
        low = lax.ppermute(
            lax.slice_in_dim(block, block.shape[dim] - width, None, axis=dim), axis, forward
        )
        high = lax.ppermute(lax.slice_in_dim(block, 0, width, axis=dim), axis, backward)
        block = jnp.concatenate([low, block, high], axis=dim)
    return block


def one_gather(arrays, axis, dims):
    line = jnp.concatenate([a.reshape(-1) for a in arrays])
    lines, at, finished = (lax.all_gather(line, axis), 0, [])
    for a, dim in zip(arrays, dims):
        parts = lines[:, at : at + a.size].reshape(-1, *a.shape)
        finished.append(laid_out(parts, dim))
        at += a.size
    return tuple(finished)


def in_one_piece(arrays, axis, dim, along):
    widths = [a.shape[along] for a in arrays]
    both = jnp.concatenate(arrays, axis=along)
    whole = lax.all_gather(both, axis, axis=dim, tiled=True)
    return tuple(jnp.split(whole, [sum(widths[:k]) for k in range(1, len(widths))], axis=along))


def layer_norm(frame_rows, ln_gain):
    widened = frame_rows.astype(jnp.float32)
    row_mean = jnp.mean(widened, axis=-1, keepdims=True)
    centered = widened - row_mean
    row_var = jnp.mean(centered * centered, axis=-1, keepdims=True)
    return (centered * lax.rsqrt(row_var + epsilon) * ln_gain).astype(jnp.bfloat16)


def sinusoid(row_count, model_width):
    offsets = jnp.arange(row_count, dtype=jnp.float32) - (row_count // 2 - 1)
    half_width = model_width // 2
    frequency = jnp.exp(
        jnp.arange(half_width, dtype=jnp.float32) * (-2.0 * math.log(10000.0) / model_width)
    )
    angles = offsets[:, None] * frequency[None, :]
    return jnp.concatenate([jnp.sin(angles), jnp.cos(angles)], axis=1).astype(jnp.bfloat16)


def rel_shift(position_full):
    block_len = position_full.shape[0]
    span_len = position_full.shape[1]
    skewed = position_full.reshape(-1)[: block_len * (span_len - 1)].reshape(
        block_len, span_len - 1
    )
    return skewed[:, block_len - 1 : 4 * block_len - 1]


def attend(
    query_proj, key_rows, value_rows, rel_heads, bias_content, bias_position, valid_len, first_pos
):
    block_len = query_proj.shape[0]
    head_count, head_size = bias_content.shape
    query_pos = first_pos + jnp.arange(block_len, dtype=jnp.int32)
    key_pos = first_pos - block_len + jnp.arange(3 * block_len, dtype=jnp.int32)
    key_valid = (key_pos >= 0) & (key_pos < valid_len)
    query_valid = (query_pos < valid_len).astype(jnp.float32)
    split_query = query_proj.reshape(block_len, head_count, head_size).astype(jnp.float32)
    with_content = (split_query + bias_content[None]).astype(jnp.bfloat16).transpose(1, 0, 2)
    with_position = (split_query + bias_position[None]).astype(jnp.bfloat16).transpose(1, 0, 2)
    key_heads = key_rows.reshape(3 * block_len, head_count, head_size).transpose(1, 0, 2)
    value_heads = value_rows.reshape(3 * block_len, head_count, head_size).transpose(1, 0, 2)
    scale = 1.0 / math.sqrt(head_size)

    def one_head(operands):
        content_query, position_query, key_head, value_head, rel_head = operands
        content = jnp.dot(content_query, key_head.T, preferred_element_type=jnp.float32)
        shifted = rel_shift(jnp.dot(position_query, rel_head.T, preferred_element_type=jnp.float32))
        scores = jnp.where(key_valid[None, :], (content + shifted) * scale, masked_score)
        row_max = jnp.max(scores, axis=1, keepdims=True)
        raised = jnp.exp(scores - row_max)
        totals = jnp.sum(raised, axis=1, keepdims=True)
        weights = (raised / totals).astype(jnp.bfloat16)
        return jnp.dot(weights, value_head, preferred_element_type=jnp.float32)

    context = lax.map(one_head, (with_content, with_position, key_heads, value_heads, rel_heads))
    context = context.transpose(1, 0, 2) * query_valid[:, None, None]
    return context.astype(jnp.bfloat16).reshape(block_len, head_count * head_size)


def column_cut(weight_shard, tm_index, tm_count):
    slice_width = weight_shard.shape[1] // tm_count
    return lax.dynamic_slice_in_dim(weight_shard, tm_index * slice_width, slice_width, 1)


def body(
    frames,
    lengths,
    ln_gain,
    w_query,
    w_key,
    w_value,
    w_output,
    w_position,
    bias_content,
    bias_position,
):
    frame_rows = frames[0]
    valid_len = lengths[0]
    block_len = frame_rows.shape[0]
    model_width = frame_rows.shape[1]
    head_count, head_size = bias_content.shape
    tm_index = lax.axis_index("tm")
    first_pos = tm_index * block_len
    normed = layer_norm(frame_rows, ln_gain)
    rel_share = jnp.dot(
        sinusoid(4 * block_len, model_width), w_position, preferred_element_type=jnp.float32
    ).astype(jnp.bfloat16)
    relative = gathered_copies(rel_share, "tm", 1)
    rel_heads = relative.reshape(4 * block_len, head_count, head_size).transpose(1, 0, 2)
    kv_source = padded(normed, (("tm", 0),), block_len)
    tm_count = lax.axis_size("tm")
    slice_query, slice_key, slice_value, slice_output = one_gather(
        (
            column_cut(w_query, tm_index, tm_count),
            column_cut(w_key, tm_index, tm_count),
            column_cut(w_value, tm_index, tm_count),
            column_cut(w_output, tm_index, tm_count),
        ),
        "dp",
        (0, 0, 0, 0),
    )
    full_query, full_key, full_value, full_output = (
        *in_one_piece((slice_query, slice_key, slice_value), "tm", 1, 0),
        lax.all_gather(slice_output, "tm", axis=1, tiled=True),
    )
    query_sum = jnp.dot(normed, full_query, preferred_element_type=jnp.float32)
    key_sum = jnp.dot(kv_source, full_key, preferred_element_type=jnp.float32)
    value_sum = jnp.dot(kv_source, full_value, preferred_element_type=jnp.float32)
    query_proj = query_sum.astype(jnp.bfloat16)
    key_proj = key_sum.astype(jnp.bfloat16)
    value_proj = value_sum.astype(jnp.bfloat16)
    context = attend(
        query_proj,
        key_proj,
        value_proj,
        rel_heads,
        bias_content,
        bias_position,
        valid_len,
        first_pos,
    )
    mixed_out = jnp.dot(context, full_output, preferred_element_type=jnp.float32)
    attended = (frame_rows.astype(jnp.float32) + mixed_out).astype(jnp.bfloat16)
    return attended[None]


def solution(mesh):
    placed = (
        P("dp", "tm", None),
        P("dp"),
        P(),
        P("dp", None),
        P("dp", None),
        P("dp", None),
        P("dp", None),
        P(None, "tm"),
        P(),
        P(),
    )
    return jax.shard_map(
        body, mesh=mesh, in_specs=placed, out_specs=P("dp", "tm", None), check_vma=False
    )
```

profile of v0, /device:TPU:25, one launch (start us, length us, event | category | flops | bytes accessed | tf_op | source)
XLA Modules:
  0.0 244.6 jit_solution(5539604920958004621)
XLA Ops:
  9.4 70.0 %all-gather = bf16[294912]{0:T(1024)(128)(2,1)S(1)} all-gather(bf16[9216]{0:T(1024)(128)(2,1)S(1)} %pad_maximum_fusion.4), channel_id=2, replica_groups=mesh['dp'=32,'tm'=16] {'dp'}, dimensions={0}, use_global_device_ids=true | all-gather | bytes 608256 | tf_op jit(solution)/shard_map/all_gather | solution.py:45
  83.6 17.5 %collective-permute-start = (bf16[256,1536]{1,0:T(8,128)(2,1)S(1)}, bf16[256,1536]{1,0:T(8,128)(2,1)S(1)}, u32[]{:S(2)}, u32[]{:S(2)}) collective-permute-start(bf16[256,1536]{1,0:T(8,128)(2,1)S(1)} %fusion.43), channel_id=1, source_target_pairs={{0,1},{1,2},{2,3},{3,4},{4,5},{5,6},{6,7},{7,8},{8,9},{9,10},{10,1... | collective-permute-start | bytes 2359304 | tf_op jit(solution)/shard_map/ppermute | solution.py:35
  101.1 1.9 collective-permute-start.1
  103.0 11.8 %fusion.24 = (bf16[1024,768]{1,0:T(8,128)(2,1)S(1)}, bf16[1024,768]{1,0:T(8,128)(2,1)S(1)}) fusion(f32[768]{0:T(1024)S(1)} %multiply_exponential_fusion, f32[1024]{0:T(1024)S(1)} %iota_add_fusion.1), kind=kLoop, calls=%fused_computation.31 | loop fusion | flops 2359296 | bytes 3152896 | tf_op jit(solution)/shard_map/convert.1
  115.9 1.3 broadcast_in_dim.22
  117.2 6.0 %all-to-all-start = ((bf16[16,1024,48]{1,2,0:T(8,128)(2,1)}), bf16[16,1024,48]{1,2,0:T(8,128)(2,1)}, u32[]{:S(2)}, u32[]{:S(2)}) async-start(bf16[16,1024,48]{1,2,0:T(8,128)(2,1)} %broadcast_in_dim.22), calls=%async_computation | async-start | bytes 3145728 | tf_op jit(solution)/shard_map/all_to_all | solution.py:14
  125.3 7.6 %collective-permute-done.1 = bf16[256,1536]{1,0:T(8,128)(2,1)} collective-permute-done((bf16[256,1536]{1,0:T(8,128)(2,1)S(1)}, bf16[256,1536]{1,0:T(8,128)(2,1)}, u32[]{:S(2)}, u32[]{:S(2)}) %collective-permute-start.1) | collective-permute-done | bytes 786464 | tf_op jit(solution)/shard_map/ppermute | solution.py:38
  132.9 33.6 %all-gather.4.cloned.1.call-done = bf16[4608,768]{0,1:T(8,128)(2,1)} async-done(((bf16[4608,48]{0,1:T(8,128)(2,1)}), bf16[4608,768]{0,1:T(8,128)(2,1)}) %all-gather.4.cloned.1.call-update) | async-done | bytes 7077904 | tf_op jit(solution)/shard_map/all_gather | solution.py:56
  166.5 4.2 %fusion.47 = bf16[768,768]{0,1:T(8,128)(2,1)S(1)} fusion(bf16[4608,768]{0,1:T(8,128)(2,1)} %all-gather.4.cloned.1.call-done, bf16[256,1536]{1,0:T(8,128)(2,1)} %collective-permute-done.1, bf16[256,1536]{1,0:T(8,128)(2,1)S(1)} %fusion.43, bf16[256,1536]{1,0:T(8,128)(2,1)} %copy-done.5), kind=kOutput, calls=%fused_computation.56 | convolution fusion | flops 1819607040 | bytes 5898240 | tf_op jit(solution)/shard_map/dot_general | solution.py:167
  170.7 1.6 copy.27
  172.2 4.2 %fusion.44 = bf16[768,768]{0,1:T(8,128)(2,1)S(1)} fusion(bf16[4608,768]{0,1:T(8,128)(2,1)} %all-gather.4.cloned.1.call-done, bf16[256,1536]{1,0:T(8,128)(2,1)} %collective-permute-done.1, bf16[256,1536]{1,0:T(8,128)(2,1)S(1)} %fusion.43, bf16[256,1536]{1,0:T(8,128)(2,1)} %copy-done.5), kind=kOutput, calls=%fused_computation.55 | convolution fusion | flops 1819607040 | bytes 5898240 | tf_op jit(solution)/shard_map/dot_general | solution.py:166
  176.4 1.6 copy.26
  178.0 2.5 %fusion.53 = f32[256,768]{1,0:T(8,128)S(1)} fusion(bf16[256,1536]{1,0:T(8,128)(2,1)S(1)} %fusion.43, bf16[4608,768]{0,1:T(8,128)(2,1)} %all-gather.4.cloned.1.call-done), kind=kOutput, calls=%fused_computation.58 | convolution fusion | flops 604372992 | bytes 3932160 | tf_op jit(solution)/shard_map/dot_general | solution.py:165
  181.8 51.4 %while.11 = (s32[]{:T(128)}, f32[8,256,96]{1,2,0:T(8,128)}, bf16[8,256,96]{1,2,0:T(8,128)(2,1)}, bf16[8,768,96]{2,1,0:T(8,128)(2,1)}, bf16[8,256,96]{1,2,0:T(8,1...) while((s32[]{:T(128)}, f32[8,256,96]{1,2,0:T(8,128)}, ...), condition=%wide.region_5.6_spmd.clone, body=%wide.region_2.5_spmd.clone.sunk | while | flops 127601152 | bytes 9182829 | solution.py:114
  184.5 1.4 fusion.81
  186.2 2.0 fusion.83
  190.9 1.4 fusion.81
  192.7 2.0 fusion.83
  197.4 1.4 fusion.81
  199.1 2.0 fusion.83
  201.1 1.2 convolution_bitcast_fusion.3
  203.8 1.4 fusion.81
  205.5 2.0 fusion.83
  210.2 1.4 fusion.81
  211.9 2.0 fusion.83
  216.6 1.4 fusion.81
  218.3 2.0 fusion.83
  223.0 1.4 fusion.81
  224.7 2.0 fusion.83
  229.5 1.4 fusion.81
  231.2 2.0 fusion.83
  234.4 3.4 %fusion.31 = bf16[1,256,1536]{2,1,0:T(8,128)(2,1)} fusion(bf16[256,768]{0,1:T(8,128)(2,1)S(1)} %bitcast.95, bf16[768,1536]{0,1:T(8,128)(2,1)} %all-gather.6.cloned.1.call-done, bf16[1,256,1536]{2,1,0:T(8,128)(2,1)S(1)} %copy-done.1), kind=kOutput, calls=%fused_computation.39 | convolution fusion | flops 605159424 | bytes 4325376 | tf_op jit(solution)/shard_map/dot_general | solution.py:181
  (90 shorter events, 34.6 us)
Async XLA Ops:
  6.5 108.3 %copy-start = (bf16[1536,48]{0,1:T(8,128)(2,1)S(1)}, bf16[1536,48]{0,1:T(8,128)(2,1)}, u32[]{:S(2)}) copy-start(bf16[1536,48]{0,1:T(8,128)(2,1)} %param.19) | copy-start | bytes 442372
  6.5 159.9 %all-gather.4.cloned.1.call-start = ((), (), s32[]{:S(2)}) async-start(), calls=%async_computation.1 | async-start | bytes 7520256 | tf_op jit(solution)/shard_map/all_gather | solution.py:56
  79.7 3.0 %copy-start.1 = (bf16[1,256,1536]{2,1,0:T(8,128)(2,1)S(1)}, bf16[1,256,1536]{2,1,0:T(8,128)(2,1)}, u32[]{:S(2)}) copy-start(bf16[1,256,1536]{2,1,0:T(8,128)(2,1)} %param.12) | copy-start | bytes 2359300
  81.0 2.3 copy-start.2
  83.6 41.7 %collective-permute-start = (bf16[256,1536]{1,0:T(8,128)(2,1)S(1)}, bf16[256,1536]{1,0:T(8,128)(2,1)S(1)}, u32[]{:S(2)}, u32[]{:S(2)}) collective-permute-start(bf16[256,1536]{1,0:T(8,128)(2,1)S(1)} %fusion.43), channel_id=1, source_target_pairs={{0,1},{1,2},{2,3},{3,4},{4,5},{5,6},{6,7},{7,8},{8,9},{9,10},{10,1... | collective-permute-start | bytes 2359304 | tf_op jit(solution)/shard_map/ppermute | solution.py:35
  101.1 31.8 %collective-permute-start.1 = (bf16[256,1536]{1,0:T(8,128)(2,1)S(1)}, bf16[256,1536]{1,0:T(8,128)(2,1)}, u32[]{:S(2)}, u32[]{:S(2)}) collective-permute-start(bf16[256,1536]{1,0:T(8,128)(2,1)S(1)} %fusion.43), channel_id=1, source_target_pairs={{1,0},{2,1},{3,2},{4,3},{5,4},{6,5},{7,6},{8,7},{9,8},{10,9},{11,1... | collective-permute-start | bytes 2359304 | tf_op jit(solution)/shard_map/ppermute | solution.py:38
  117.2 64.6 %all-to-all-start = ((bf16[16,1024,48]{1,2,0:T(8,128)(2,1)}), bf16[16,1024,48]{1,2,0:T(8,128)(2,1)}, u32[]{:S(2)}, u32[]{:S(2)}) async-start(bf16[16,1024,48]{1,2,0:T(8,128)(2,1)} %broadcast_in_dim.22), calls=%async_computation | async-start | bytes 3145728 | tf_op jit(solution)/shard_map/all_to_all | solution.py:14
  123.3 111.1 %all-gather.6.cloned.1.call-start = ((), (), s32[]{:S(2)}) async-start(), calls=%async_computation.2 | async-start | bytes 2506752 | tf_op jit(solution)/shard_map/all_gather | solution.py:163
  125.3 7.6 %copy-start.5 = (bf16[256,1536]{1,0:T(8,128)(2,1)}, bf16[256,1536]{1,0:T(8,128)(2,1)S(1)}, u32[]{:S(2)}) copy-start(bf16[256,1536]{1,0:T(8,128)(2,1)S(1)} %collective-permute-done) | copy-start | bytes 2359300
  178.0 2.8 %copy-start.3 = (f32[8,96]{1,0:T(8,128)S(1)}, f32[8,96]{1,0:T(8,128)}, u32[]{:S(2)}) copy-start(f32[8,96]{1,0:T(8,128)} %param.21) | copy-start | bytes 9220
  178.0 2.8 %copy-start.4 = (f32[8,96]{1,0:T(8,128)S(1)}, f32[8,96]{1,0:T(8,128)}, u32[]{:S(2)}) copy-start(f32[8,96]{1,0:T(8,128)} %param.20) | copy-start | bytes 9220
Sparse Core Ops, SparseCore 0:
  82.8 83.6 all-gather.3
  168.6 33.9 all-gather.5
where the time goes:
time: 247 us; the launch traced here: 245 us
  blocking collectives  70 us (28%)
  matrix products  52.3 us (21%)
  waiting for transfers between devices  41.2 us (17%)
  starting transfers between devices  25.7 us (10%)
  other arithmetic  23.1 us (9%)
  local copies, waits for them, and re-layouts  17.7 us (7%)
  between operations  14.3 us (6%)
    all_gather x1, blocking collectives, one_gather(): lines, at, finished = (lax.all_gather(line, axis), 0, [])  70 us
    all_gather x1, waiting for transfers between devices, in_one_piece(): whole = lax.all_gather(both, axis, axis=dim, tiled=True)  33.6 us
    ppermute x1, starting transfers between devices, padded(): lax.ppermute(lax.slice_in_dim(block, block.shape[dim] - width, None, axis...  17.5 us
    dot_general x8, matrix products, one_head(): return jnp.dot(weights, value_head, preferred_element_type=jnp.float32)  15.8 us
    another operation x1, other arithmetic  11.8 us
    dot_general x8, matrix products, one_head(): jnp.dot(content_query, key_head.T, preferred_element_type=jnp.float32)  11.3 us
    dot_general x8, matrix products, one_head(): jnp.dot(position_query, rel_head.T, preferred_element_type=jnp.float32)  9.93 us
    ppermute x1, waiting for transfers between devices, padded(): lax.ppermute(lax.slice_in_dim(block, 0, width, axis=dim), axis, backward)  7.6 us
  transfers between devices with their start and end apart: 5, of which 2 were waited for; matrix products, arithmetic and copies ran while one was open for 34% of the time, Pallas kernels for 0%

commit v1 on v0

v1 whole, which is shorter than its diff:
```python
import math

import jax
import jax.numpy as jnp
from jax import lax
from jax.experimental import pallas as pl
from jax.experimental.pallas import tpu as pltpu
from jax.sharding import PartitionSpec as P

MESH = pl.DeviceIdType.MESH
epsilon = 1e-05
masked_score = -1e30
BF16 = jnp.bfloat16
F32 = jnp.float32

D = 1536
HS = 96
BLOCK = 256
HALF = 384
NX = 4
NY = 4
STEP_ROWS = 128
GROUP = 32


def mm(a, b):
    return jnp.dot(a, b, preferred_element_type=F32)


def mm_t(a, b):
    return lax.dot_general(a, b, (((1,), (1,)), ((), ())), preferred_element_type=F32)


def kernel(
    nz,
    frames_ref,
    len_ref,
    gain_ref,
    wq_ref,
    wk_ref,
    wv_ref,
    wo_ref,
    wpos_ref,
    bias_ref,
    table_ref,
    out_ref,
    normed,
    pack,
    packo,
    big,
    bigo,
    enc,
    rel_own,
    rel,
    keys,
    values,
    with_c,
    with_p,
    ctx_out,
    ctx,
    loc_sem,
    s0_send,
    s0_recv,
    zs,
    zr,
    xs,
    xr,
    ys,
    yr,
    ra_send,
    ra_recv,
    rx_send,
    rx_recv,
    h_send,
    h_recv,
    p_send,
    p_recv,
):
    dp = lax.axis_index("dp")
    tm = lax.axis_index("tm")
    y_hi = dp // nz
    z = dp % nz
    y_lo = tm // 8
    x = (tm % 8) // 2
    c = tm % 2
    y = y_hi * 2 + y_lo
    half = nz // 2

    def dev(xx, yy, zz, cc):
        return ((yy // 2) * nz + zz, (yy % 2) * 8 + xx * 2 + cc)

    x_r, x_l, x_o = (x + 1) % NX, (x + 3) % NX, (x + 2) % NX
    y_r, y_l, y_o = (y + 1) % NY, (y + 3) % NY, (y + 2) % NY
    z_r, z_l = (z + 1) % nz, (z + nz - 1) % nz
    y_mate = y_hi * 2 + (1 - y_lo)
    y_mirror = 3 - y
    place = y_lo * NX + x
    nxt, prv = (place + 1) % 8, (place + 7) % 8
    dev_next = dev(nxt % NX, y_hi * 2 + nxt // NX, z, c)
    dev_prev = dev(prv % NX, y_hi * 2 + prv // NX, z, c)
    partner = dev(x, y, z, 1 - c)

    locals_ = []
    base = pl.multiple_of(c * HALF, 128)
    for k, ref in enumerate((wq_ref, wk_ref, wv_ref)):
        for j in range(3):
            t = 3 * k + j
            locals_.append(
                pltpu.make_async_copy(
                    ref.at[:, pl.ds(base + 128 * j, 128)], pack.at[t], loc_sem.at[t]
                )
            )
    baseo = pl.multiple_of(c * 768, 128)
    for j in range(6):
        locals_.append(
            pltpu.make_async_copy(
                wo_ref.at[:, pl.ds(baseo + 128 * j, 128)], packo.at[j], loc_sem.at[9 + j]
            )
        )
    for cp in locals_:
        cp.start()

    barrier = pltpu.get_barrier_semaphore()
    peers = [
        dev(x_r, y, z, c),
        dev(x_l, y, z, c),
        dev(x, y_r, z, c),
        dev(x, y_l, z, c),
        dev(x, y, z_r, c),
        dev(x, y, z_l, c),
        partner,
        dev(x, y_mate, z, 1 - c),
        dev_next,
        dev_prev,
    ]
    for p in peers:
        pl.semaphore_signal(barrier, inc=1, device_id=p, device_id_type=MESH)

    for cp in locals_:
        cp.wait()
    pl.semaphore_wait(barrier, len(peers))

    def rows(zz):
        return pl.ds(pl.multiple_of(zz * 48, 16), 48)

    def orows(zz):
        return pl.ds(pl.multiple_of(zz * 24, 8), 24)

    own_tiles = (x, NX + y, 8)
    mir_tiles = (x, NX + y_mirror, 8)
    own_o = (y, 4, 5)
    mir_o = (y_mirror, 4, 5)
    mirror = dev(x, y_mirror, z, c)
    stage0 = []
    own_copies = []
    for i in range(3):
        stage0.append(
            pltpu.make_async_remote_copy(
                pack.at[mir_tiles[i]],
                big.at[mir_tiles[i], y_hi, rows(z), :],
                s0_send.at[i],
                s0_recv.at[i],
                device_id=mirror,
                device_id_type=MESH,
            )
        )
        stage0.append(
            pltpu.make_async_remote_copy(
                packo.at[mir_o[i]],
                bigo.at[c, mir_o[i], y_hi, orows(z), :],
                s0_send.at[3 + i],
                s0_recv.at[3 + i],
                device_id=mirror,
                device_id_type=MESH,
            )
        )
        own_copies.append(
            pltpu.make_async_copy(
                pack.at[own_tiles[i]], big.at[own_tiles[i], y_hi, rows(z), :], loc_sem.at[i]
            )
        )
        own_copies.append(
            pltpu.make_async_copy(
                packo.at[own_o[i]], bigo.at[c, own_o[i], y_hi, orows(z), :], loc_sem.at[3 + i]
            )
        )
    for cp in stage0:
        cp.start()
    for cp in own_copies:
        cp.start()

    widened = frames_ref[...].astype(F32)
    row_mean = jnp.mean(widened, axis=-1, keepdims=True)
    centered = widened - row_mean
    row_var = jnp.mean(centered * centered, axis=-1, keepdims=True)
    own_rows = pl.ds(pl.multiple_of(c * BLOCK, BLOCK), BLOCK)
    normed[own_rows, :] = (centered * lax.rsqrt(row_var + epsilon) * gain_ref[...]).astype(BF16)
    send_normed = pltpu.make_async_remote_copy(
        normed.at[own_rows, :],
        normed.at[own_rows, :],
        p_send.at[0],
        p_recv.at[0],
        device_id=partner,
        device_id_type=MESH,
    )
    send_normed.start()

    for cp in own_copies:
        cp.wait()
    for i in range(3):
        pltpu.make_async_remote_copy(
            pack.at[own_tiles[i]],
            big.at[own_tiles[i], 1 - y_hi, rows(z), :],
            s0_send.at[i],
            s0_recv.at[i],
            device_id=mirror,
            device_id_type=MESH,
        ).wait_recv()
        pltpu.make_async_remote_copy(
            packo.at[own_o[i]],
            bigo.at[c, own_o[i], 1 - y_hi, orows(z), :],
            s0_send.at[3 + i],
            s0_recv.at[3 + i],
            device_id=mirror,
            device_id_type=MESH,
        ).wait_recv()

    def zview(lane, zz):
        if lane < 3:
            return big.at[own_tiles[lane], :, rows(zz), :]
        if lane == 3:
            return bigo.at[c, y, :, orows(zz), :]
        return bigo.at[c, 4:6, :, orows(zz), :]

    def zcopy(lane, way, zz):
        view = zview(lane, zz)
        return pltpu.make_async_remote_copy(
            view,
            view,
            zs.at[way, lane, zz],
            zr.at[lane, zz],
            device_id=dev(x, y, z_r if way == 0 else z_l, c),
            device_id_type=MESH,
        )

    def xcopy(kind, tile, zz, to):
        view = big.at[tile, :, rows(zz), :]
        return pltpu.make_async_remote_copy(
            view,
            view,
            xs.at[kind, zz],
            xr.at[kind, zz],
            device_id=dev(to, y, z, c),
            device_id_type=MESH,
        )

    def ycopy(lane, kind, tile, zz, to):
        view = big.at[NX + tile, :, rows(zz), :] if lane == 0 else bigo.at[c, tile, :, orows(zz), :]
        return pltpu.make_async_remote_copy(
            view,
            view,
            ys.at[lane, kind, zz],
            yr.at[lane, kind, zz],
            device_id=dev(x, to, z, c),
            device_id_type=MESH,
        )

    def spread(zz):
        xcopy(0, x, zz, x_r).start()
        xcopy(1, x, zz, x_l).start()
        for lane in range(2):
            ycopy(lane, 0, y, zz, y_r).start()
            ycopy(lane, 1, y, zz, y_l).start()

    def pass_on(way, zz):
        if way == 0:
            xcopy(0, x_l, zz, x_r).wait_recv()
            xcopy(2, x_l, zz, x_r).start()
            for lane in range(2):
                ycopy(lane, 0, y_l, zz, y_r).wait_recv()
                ycopy(lane, 2, y_l, zz, y_r).start()
        else:
            xcopy(1, x_r, zz, x_l).wait_recv()
            xcopy(2, x_r, zz, x_l).start()
            for lane in range(2):
                ycopy(lane, 1, y_r, zz, y_l).wait_recv()
                ycopy(lane, 2, y_r, zz, y_l).start()

    def rel_piece(s):
        for g in range(STEP_ROWS // GROUP):
            i = s * (STEP_ROWS // GROUP) + g
            sa = table_ref[0, pl.ds(i, 1), :]
            ca = table_ref[1, pl.ds(i, 1), :]
            sb = table_ref[2]
            cb = table_ref[3]
            enc[g * GROUP : (g + 1) * GROUP, 0:768] = (sa * cb + ca * sb).astype(BF16)
            enc[g * GROUP : (g + 1) * GROUP, 768:1536] = (ca * cb - sa * sb).astype(BF16)
        piece = mm(enc[...], wpos_ref[...])
        rel_own[:, pl.ds(pl.multiple_of(s * STEP_ROWS, STEP_ROWS), STEP_ROWS)] = piece.T.astype(BF16)

    pieces = 1024 // STEP_ROWS

    def step(s, carry):
        up = (z + nz - s) % nz
        down = (z + s) % nz
        for lane in range(5):

            @pl.when(s > 0)
            def _():
                zcopy(lane, 0, up).wait_recv()

            @pl.when(s < half)
            def _():
                zcopy(lane, 0, up).start()

            @pl.when((s > 0) & (s < half))
            def _():
                zcopy(lane, 1, down).wait_recv()

            @pl.when(s < half - 1)
            def _():
                zcopy(lane, 1, down).start()

        spread(up)

        @pl.when((s > 0) & (s < half))
        def _():
            spread(down)

        @pl.when(s > 0)
        def _():
            pass_on(0, (z + nz - s + 1) % nz)

        @pl.when(s > 1)
        def _():
            pass_on(1, (z + s - 1) % nz)

        @pl.when(s < pieces)
        def _():
            rel_piece(s)

        return carry

    lax.fori_loop(0, half + 1, step, 0)
    pass_on(0, (z + half) % nz)

    slot = pl.ds(pl.multiple_of(x * HS + c * 48, 16), 48)
    rel_cross = pltpu.make_async_remote_copy(
        rel_own,
        rel.at[slot, :],
        ra_send.at[0],
        ra_recv.at[c],
        device_id=dev(x, y_mate, z, y_lo),
        device_id_type=MESH,
    )
    rel_cross.start()
    rel_here = pltpu.make_async_copy(rel_own, rel.at[slot, :], loc_sem.at[0])
    rel_across = pltpu.make_async_remote_copy(
        rel_own,
        rel.at[slot, :],
        ra_send.at[1],
        ra_recv.at[c],
        device_id=partner,
        device_id_type=MESH,
    )

    @pl.when(c == y_lo)
    def _():
        rel_here.start()

    @pl.when(c != y_lo)
    def _():
        rel_across.start()

    def collect(zz, carry):
        offset = (zz + nz - z) % nz
        is_up = (offset == 0) | (offset >= half)

        @pl.when(is_up)
        def _():
            xcopy(1, x_r, zz, x_l).wait_recv()
            for lane in range(2):
                ycopy(lane, 1, y_r, zz, y_l).wait_recv()

        @pl.when(jnp.logical_not(is_up))
        def _():
            xcopy(0, x_l, zz, x_r).wait_recv()
            for lane in range(2):
                ycopy(lane, 0, y_l, zz, y_r).wait_recv()

        xcopy(2, x_o, zz, x_r).wait_recv()
        for lane in range(2):
            ycopy(lane, 2, y_o, zz, y_r).wait_recv()
        return carry

    lax.fori_loop(0, nz, collect, 0)

    send_o = pltpu.make_async_remote_copy(
        bigo.at[c], bigo.at[c], p_send.at[1], p_recv.at[1], device_id=partner, device_id_type=MESH
    )
    send_o.start()
    send_normed.wait_recv()

    def weight(t):
        return jnp.concatenate([big[t + j].reshape(D, 128) for j in range(3)], axis=1)

    def project(t, row):
        return mm(normed[pl.ds(row, BLOCK), :], weight(t))

    for b in range(2):
        keys[BLOCK * (b + 1) : BLOCK * (b + 2), :] = project(3, BLOCK * b).astype(BF16)
        values[BLOCK * (b + 1) : BLOCK * (b + 2), :] = project(6, BLOCK * b).astype(BF16)

    first, last = place == 0, place == 7
    halos = []
    for k, ref in enumerate((keys, values)):
        halos.append(
            pltpu.make_async_remote_copy(
                ref.at[pl.ds(BLOCK, BLOCK), :],
                ref.at[pl.ds(3 * BLOCK, BLOCK), :],
                h_send.at[k, 0],
                h_recv.at[k, 0],
                device_id=dev_prev,
                device_id_type=MESH,
            )
        )
        halos.append(
            pltpu.make_async_remote_copy(
                ref.at[pl.ds(2 * BLOCK, BLOCK), :],
                ref.at[pl.ds(0, BLOCK), :],
                h_send.at[k, 1],
                h_recv.at[k, 1],
                device_id=dev_next,
                device_id_type=MESH,
            )
        )

    @pl.when(jnp.logical_not(first))
    def _():
        halos[0].start()
        halos[2].start()

    @pl.when(jnp.logical_not(last))
    def _():
        halos[1].start()
        halos[3].start()

    @pl.when(first)
    def _():
        keys[0:BLOCK, :] = jnp.zeros((BLOCK, HALF), BF16)
        values[0:BLOCK, :] = jnp.zeros((BLOCK, HALF), BF16)

    @pl.when(last)
    def _():
        keys[3 * BLOCK : 4 * BLOCK, :] = jnp.zeros((BLOCK, HALF), BF16)
        values[3 * BLOCK : 4 * BLOCK, :] = jnp.zeros((BLOCK, HALF), BF16)

    bias_c = bias_ref[pl.ds(c, 1), :]
    bias_p = bias_ref[pl.ds(2 + c, 1), :]
    for b in range(2):
        query = project(0, BLOCK * b).astype(BF16).astype(F32)
        with_c[BLOCK * b : BLOCK * (b + 1), :] = (query + bias_c).astype(BF16)
        with_p[BLOCK * b : BLOCK * (b + 1), :] = (query + bias_p).astype(BF16)

    def rcopy(kind, row, count, to):
        view = rel.at[pl.ds(pl.multiple_of(row, 16), count), :]
        return pltpu.make_async_remote_copy(
            view,
            view,
            rx_send.at[kind],
            rx_recv.at[kind],
            device_id=dev(to, y, z, c),
            device_id_type=MESH,
        )

    @pl.when(c == y_lo)
    def _():
        rel_here.wait()

    def rel_wait(core):
        pltpu.make_async_remote_copy(
            rel_own,
            rel.at[pl.ds(pl.multiple_of(x * HS + core * 48, 16), 48), :],
            ra_send.at[0],
            ra_recv.at[core],
            device_id=partner,
            device_id_type=MESH,
        ).wait_recv()

    rel_wait(1 - c)

    @pl.when(c != y_lo)
    def _():
        rel_wait(c)

    rcopy(0, x * HS, HS, x_r).start()
    rcopy(1, x * HS, HS, x_l).start()
    rcopy(0, x_l * HS, HS, x_r).wait_recv()
    rcopy(2, x_l * HS, 48, x_r).start()
    rcopy(1, x_r * HS, HS, x_l).wait_recv()
    rcopy(3, x_r * HS + 48, 48, x_l).start()
    rcopy(2, x_o * HS, 48, x_r).wait_recv()
    rcopy(3, x_o * HS + 48, 48, x_l).wait_recv()

    @pl.when(jnp.logical_not(last))
    def _():
        halos[0].wait_recv()
        halos[2].wait_recv()

    @pl.when(jnp.logical_not(first))
    def _():
        halos[1].wait_recv()
        halos[3].wait_recv()

    valid_len = len_ref[0]
    scale = 1.0 / math.sqrt(HS)
    windows = ((0, 128), (0, 256), (128, 384), (256, 384))
    send_ctx = pltpu.make_async_remote_copy(
        ctx_out, ctx.at[c], p_send.at[2], p_recv.at[2], device_id=partner, device_id_type=MESH
    )

    def attend(i, carry):
        b = jnp.where(i == 0, 1 - c, c)
        row = pl.multiple_of(b * BLOCK, BLOCK)
        first_pos = place * (2 * BLOCK) + row
        key_pos = first_pos - BLOCK + lax.broadcasted_iota(jnp.int32, (1, 3 * BLOCK), 1)
        key_valid = (key_pos >= 0) & (key_pos < valid_len)
        query_pos = first_pos + lax.broadcasted_iota(jnp.int32, (BLOCK, 1), 0)
        parts = []
        for h, (lo, hi) in enumerate(windows):
            lane = lo + lax.broadcasted_iota(jnp.int32, (BLOCK, hi - lo), 1)
            mine = (lane >= HS * h) & (lane < HS * (h + 1))
            zero = jnp.zeros((BLOCK, hi - lo), BF16)
            qc = jnp.where(mine, with_c[pl.ds(row, BLOCK), lo:hi], zero)
            qp = jnp.where(mine, with_p[pl.ds(row, BLOCK), lo:hi], zero)
            position = mm(qp, rel[lo:hi, :])
            shifted = pltpu.roll(position, 3 * BLOCK + 1, 1, stride=1, stride_axis=0)[:, : 3 * BLOCK]
            score = mm_t(qc, keys[pl.ds(row, 3 * BLOCK), lo:hi]) + shifted
            score = jnp.where(key_valid, score, masked_score)
            raised = jnp.exp((score - jnp.max(score, axis=1, keepdims=True)) * scale)
            total = jnp.sum(raised, axis=1, keepdims=True)
            inverse = jnp.where(query_pos < valid_len, 1.0 / total, 0.0)
            parts.append(mm(raised.astype(BF16), values[pl.ds(row, 3 * BLOCK), lo:hi]) * inverse)
        lane = lax.broadcasted_iota(jnp.int32, (BLOCK, 128), 1)
        tiles = (
            jnp.where(lane < 96, parts[0], parts[1][:, :128]),
            jnp.where(lane < 64, parts[1][:, 128:], parts[2][:, :128]),
            jnp.where(lane < 32, parts[2][:, 128:], parts[3]),
        )

        @pl.when(i == 0)
        def _():
            for j, tile in enumerate(tiles):
                ctx_out[:, 128 * j : 128 * (j + 1)] = tile.astype(BF16)
            send_ctx.start()

        @pl.when(i == 1)
        def _():
            for j, tile in enumerate(tiles):
                ctx[c, :, 128 * j : 128 * (j + 1)] = tile.astype(BF16)

        return carry

    lax.fori_loop(0, 2, attend, 0)

    pltpu.make_async_remote_copy(
        bigo.at[1 - c],
        bigo.at[1 - c],
        p_send.at[1],
        p_recv.at[1],
        device_id=partner,
        device_id_type=MESH,
    ).wait_recv()
    pltpu.make_async_remote_copy(
        ctx_out, ctx.at[1 - c], p_send.at[2], p_recv.at[2], device_id=partner, device_id_type=MESH
    ).wait_recv()

    for g in range(2):
        for j in range(0, 6, 2):
            total = None
            for k in range(2):
                w = jnp.concatenate([bigo[g, j, k], bigo[g, j + 1, k]], axis=1)
                part = mm(ctx[k], w)
                total = part if total is None else total + part
            at = g * 768 + j * 128
            out_ref[:, at : at + 256] = (frames_ref[:, at : at + 256].astype(F32) + total).astype(BF16)

    for cp in stage0:
        cp.wait_send()
    send_normed.wait_send()
    send_o.wait_send()
    send_ctx.wait_send()
    rel_cross.wait_send()

    @pl.when(c != y_lo)
    def _():
        rel_across.wait_send()

    rcopy(0, x * HS, HS, x_r).wait_send()
    rcopy(1, x * HS, HS, x_l).wait_send()
    rcopy(2, x_l * HS, 48, x_r).wait_send()
    rcopy(3, x_r * HS + 48, 48, x_l).wait_send()

    @pl.when(jnp.logical_not(first))
    def _():
        halos[0].wait_send()
        halos[2].wait_send()

    @pl.when(jnp.logical_not(last))
    def _():
        halos[1].wait_send()
        halos[3].wait_send()

    def drain(zz, carry):
        offset = (zz + nz - z) % nz
        is_up = (offset == 0) | (offset > half)
        for lane in range(5):

            @pl.when(is_up)
            def _():
                zcopy(lane, 0, zz).wait_send()

            @pl.when(offset < half - 1)
            def _():
                zcopy(lane, 1, zz).wait_send()

        for kind in range(3):
            xcopy(kind, x, zz, x_r).wait_send()
            for lane in range(2):
                ycopy(lane, kind, y, zz, y_r).wait_send()
        return carry

    lax.fori_loop(0, nz, drain, 0)


def attention_block(nz, frames, lengths, gain, wq, wk, wv, wo, wpos, bias, table):
    vmem = pl.BlockSpec(memory_space=pltpu.VMEM)
    hbm = pl.BlockSpec(memory_space=pl.ANY)
    smem = pl.BlockSpec(memory_space=pltpu.SMEM)
    dma = pltpu.SemaphoreType.DMA
    rows = nz * 48
    return pl.pallas_call(
        lambda *refs: kernel(nz, *refs),
        out_shape=jax.ShapeDtypeStruct((BLOCK, D), BF16),
        in_specs=[vmem, smem, vmem, hbm, hbm, hbm, hbm, vmem, vmem, vmem],
        out_specs=vmem,
        scratch_shapes=[
            pltpu.VMEM((2 * BLOCK, D), BF16),
            pltpu.VMEM((9, 48, 128), BF16),
            pltpu.VMEM((6, 24, 128), BF16),
            pltpu.VMEM((9, 2, rows, 128), BF16),
            pltpu.VMEM((2, 6, 2, nz * 24, 128), BF16),
            pltpu.VMEM((STEP_ROWS, D), BF16),
            pltpu.VMEM((48, 1024), BF16),
            pltpu.VMEM((HALF, 1024), BF16),
            pltpu.VMEM((4 * BLOCK, HALF), BF16),
            pltpu.VMEM((4 * BLOCK, HALF), BF16),
            pltpu.VMEM((2 * BLOCK, HALF), BF16),
            pltpu.VMEM((2 * BLOCK, HALF), BF16),
            pltpu.VMEM((BLOCK, HALF), BF16),
            pltpu.VMEM((2, BLOCK, HALF), BF16),
            dma((15,)),
            dma((6,)),
            dma((6,)),
            dma((2, 5, nz)),
            dma((5, nz)),
            dma((3, nz)),
            dma((3, nz)),
            dma((2, 3, nz)),
            dma((2, 3, nz)),
            dma((2,)),
            dma((2,)),
            dma((4,)),
            dma((4,)),
            dma((2, 2)),
            dma((2, 2)),
            dma((3,)),
            dma((3,)),
        ],
        compiler_params=pltpu.CompilerParams(
            collective_id=0, has_side_effects=True, vmem_limit_bytes=60 * 1024 * 1024
        ),
        name="attention_block",
    )(frames, lengths, gain, wq, wk, wv, wo, wpos, bias, table)


def angle_tables():
    frequency = jnp.exp(jnp.arange(D // 2, dtype=F32) * (-2.0 * math.log(10000.0) / D))
    steps = jnp.arange(GROUP, dtype=F32)
    coarse = (steps * GROUP - (2 * BLOCK - 1))[:, None] * frequency[None, :]
    fine = steps[:, None] * frequency[None, :]
    return jnp.stack([jnp.sin(coarse), jnp.cos(coarse), jnp.sin(fine), jnp.cos(fine)])


def solution(mesh):
    nz = mesh.shape["dp"] // 2

    def body(
        frames, lengths, ln_gain, w_query, w_key, w_value, w_output, w_position, bias_c, bias_p
    ):
        bias = jnp.concatenate([bias_c.reshape(2, HALF), bias_p.reshape(2, HALF)])
        out = attention_block(
            nz,
            frames[0],
            lengths,
            ln_gain.reshape(1, D),
            w_query,
            w_key,
            w_value,
            w_output,
            w_position,
            bias,
            angle_tables(),
        )
        return out[None]

    placed = (
        P("dp", "tm", None),
        P("dp"),
        P(),
        P("dp", None),
        P("dp", None),
        P("dp", None),
        P("dp", None),
        P(None, "tm"),
        P(),
        P(),
    )
    return jax.shard_map(
        body, mesh=mesh, in_specs=placed, out_specs=P("dp", "tm", None), check_vma=False
    )
```

time: 247 us -> 91.1 us (0.37)
  the two profiles are of different devices: /device:TPU:25 before, /device:TPU:2 now
where the time goes in v1:
time: 91.1 us; the launch traced here: 90.7 us
  Pallas kernels  83.3 us (91%)
  local copies, waits for them, and re-layouts  4.57 us (5%)
  other arithmetic  2.12 us (2%)
    pallas_call x1, Pallas kernels, attention_block(): pl.pallas_call(lambda *refs: kernel(nz, *refs), out_shape=jax.ShapeDtypeS...  83.3 us
    unnamed x10, local copies, waits for them, and re-layouts  3.82 us

profile of v1, /device:TPU:2, one launch (start us, length us, event | category | flops | bytes accessed | tf_op | source)
XLA Modules:
  0.0 90.7 jit_solution(890404816296083766)
XLA Ops:
  0.0 0.0 copy-start.2
  0.7 0.0 copy-start.3
  0.7 0.0 copy-done.2
  0.7 0.1 reshape.169
  0.8 0.6 copy-done.3
  1.4 0.1 reshape.170
  1.4 0.0 copy-start.1
  1.4 0.6 pad_maximum_fusion.1.refs_8_
  2.0 0.1 copy-done.1
  2.1 0.6 reshape.168.refs_2_
  2.7 0.7 multiply_sine_fusion
  3.4 0.0 copy-start
  3.5 0.8 pad_maximum_fusion.refs_9_
  4.2 0.2 copy-done
  4.4 0.9 %copy.11.refs_7_ = bf16[1536,48]{1,0:T(8,128)(2,1)} copy(bf16[1536,48]{0,1:T(8,128)(2,1)S(1)} %copy-done) | data formatting | bytes 294912 | tf_op args[7]
  5.3 83.3 %attention_block.1 = bf16[256,1536]{1,0:T(8,128)(2,1)} custom-call(bf16[256,1536]{1,0:T(8,128)(2,1)} %bitcast.3, s32[1]{0:T(128)S(6)} %copy.13.refs_1_, f32[1,1536]{1,0:T(1,128)} %reshape.168.refs_2_, bf16[48,768]{1,0:T(8,128)(2,1)} %refs_3_.1, bf16[48,768]{1,0:T(8,128)(2,1)} %refs_4_.1, bf16[48,768]{1,0:T(8,128)(2,1)} %refs_5_.1, bf16[24,1536]{1,0:T(8,128)(2,1)} %refs_6_.1, ...), custom_call_target="tpu_custom_call" | custom-call | tf_op jit(solution)/shard_map/attention_block/pallas_call | solution.py:642
  88.6 2.1 %copy.14 = bf16[1,256,1536]{2,1,0:T(8,128)(2,1)} copy(bf16[1,256,1536]{2,1,0:T(8,128)(2,1)} %bitcast.2) | data formatting | bytes 1572864
  (2 shorter events, 0.0 us)
Async XLA Ops:
  0.0 0.7 copy-start.2
  0.7 0.7 copy-start.3
  1.4 0.7 copy-start.1
  3.4 1.0 %copy-start = (bf16[1536,48]{0,1:T(8,128)(2,1)S(1)}, bf16[1536,48]{0,1:T(8,128)(2,1)}, u32[]{:S(2)}) copy-start(bf16[1536,48]{0,1:T(8,128)(2,1)} %param.17) | copy-start | bytes 442372
